TPU v7x, 32 devices: a whole 2x2x4 slice. The times are simulated.
32 devices in a mesh: copy: 2 (over x), tm: 2 (over core), space: 8 (over z, y).
Axes of the slice: x: 2, y: 2, z: 4, core: 2. Of those that a mesh axis runs over, the one named last changes fastest.
Arguments:
- initial: float32 [4, 16, 128, 128], P(('copy', 'tm'), 'space'), parts along dimension 0, may hold values from 0.1 to 2
- source: bfloat16 [4, 16, 128, 128], P(('copy', 'tm'), 'space'), parts along dimension 0, may hold values from 0.049804688 to 1
- diffusion: float32 [16, 128, 128], P('space'), may hold values from 0.02 to 0.5
- wind_field: float32 [3, 16, 128, 128], P(None, 'space'), may hold values from -0.6 to 0.6
- buildings: int32 [16, 128, 128], P('space'), may hold values from 0 to 1, as said below
- strength: float32 [2, 4], P('tm'), may hold values from 0.5 to 2
Outputs:
- advanced: float32 [4, 16, 128, 128], P(('copy', 'tm'), 'space'), parts along dimension 0
- final_fine: float32 [4, 16, 128, 128], P(('copy', 'tm'), 'space'), parts along dimension 0
There are 2 independent parts, one for each index of `copy`. A program takes and returns all parts, laid end to end along the dimension named above; an argument that names none is the same for every part. Nothing has to cross between parts.
Inputs may be any that keep to these rules, and one draw needn't show every extreme that they name: buildings stand on the ground as columns.
All inputs are finite; a program needn't handle non-finite values.
Results may differ from a plain program's by a relative error of at most 0.0003.
Values sent between devices are 32-bit elements; how exact they have to be, the bound alone decides.
A program may use at most 64 MiB of HBM per device.

v0:
```python
import jax
import jax.numpy as jnp
from jax import lax
from jax.sharding import PartitionSpec as P

FINE = 4


lower_bound = 0.5


def extended(block, sides, width):
    for axis, dim in sides:
        count = lax.axis_size(axis)
        forward = [(i, i + 1) for i in range(count - 1)]
        backward = [(target, source) for source, target in forward]
        low = lax.ppermute(
            lax.slice_in_dim(block, block.shape[dim] - width, None, axis=dim), axis, forward
        )
        high = lax.ppermute(lax.slice_in_dim(block, 0, width, axis=dim), axis, backward)
        block = jnp.concatenate([low, block, high], axis=dim)
    return block


def shifted(array, axis, by):
    peers = lax.axis_size(axis)
    pairs = [(i, i + by) for i in range(peers) if 0 <= i + by < peers]
    return lax.ppermute(array, axis, pairs)


def ahead(values, direction):
    length = values.shape[direction]
    tail = lax.slice_in_dim(values, 1, length, axis=direction)
    blank = jnp.zeros_like(lax.slice_in_dim(values, 0, 1, axis=direction))
    return jnp.concatenate([tail, blank], axis=direction)


def behind(values, direction):
    length = values.shape[direction]
    head = lax.slice_in_dim(values, 0, length - 1, axis=direction)
    blank = jnp.zeros_like(lax.slice_in_dim(values, 0, 1, axis=direction))
    return jnp.concatenate([blank, head], axis=direction)


def face_terms(masked, winds):
    opened = jnp.where(masked > 0.0, 1.0, 0.0).astype(masked.dtype)
    result = []
    for direction in range(3):
        conduct = jnp.sqrt(masked * ahead(masked, direction))
        velocity = (
            0.5
            * (winds[direction] + ahead(winds[direction], direction))
            * opened
            * ahead(opened, direction)
        )
        result.append((conduct, velocity))
    return tuple(result)


def disk_fields(face_set):
    conduct_sum = jnp.zeros_like(face_set[0][0])
    speed_sum = jnp.zeros_like(face_set[0][0])
    for direction in range(3):
        conduct, velocity = face_set[direction]
        speed = jnp.abs(velocity)
        conduct_sum = conduct_sum + conduct + behind(conduct, direction)
        speed_sum = speed_sum + speed + behind(speed, direction)
    return (conduct_sum, speed_sum)


def operate(values, face_set, rate):
    total = values
    for direction in range(3):
        conduct, velocity = face_set[direction]
        neighbor = ahead(values, direction)
        flowing = conduct * (values - neighbor) + rate * (
            jnp.maximum(velocity, 0.0) * values + jnp.minimum(velocity, 0.0) * neighbor
        )
        total = total + flowing - behind(flowing, direction)
    return total


def coefficients(bound):
    theta = (bound + lower_bound) * 0.5
    delta = (bound - lower_bound) * 0.5
    sigma = theta / delta
    rho_one = 1.0 / sigma
    rho_two = 1.0 / (2.0 * sigma - rho_one)
    return (theta, delta, rho_one, rho_two)


def shards(initial, source, diffusion, wind_field, buildings, strength):
    opened = (1 - buildings).astype(jnp.float32)
    masked = diffusion * opened
    forcing = source[0].astype(jnp.float32) * opened
    rates = strength[0]
    margin = 2
    stacked = jnp.stack([masked, wind_field[0], wind_field[1], wind_field[2], forcing])
    border = extended(stacked, (("space", 1),), 2)
    face_set = face_terms(border[0], (border[1], border[2], border[3]))
    inner_set = tuple(((pair[0][1:-1], pair[1][1:-1]) for pair in face_set))
    forcing_ext = border[4]
    conduct_sum, speed_sum = disk_fields(face_set)
    conduct_sum = conduct_sum[margin:-margin]
    speed_sum = speed_sum[margin:-margin]

    def advance(current, fine_step, bound):
        rate = rates[fine_step]
        theta, delta, rho_one, rho_two = coefficients(bound)
        widened = extended(current, (("space", 0),), 2)
        residual = widened[1:-1] + forcing_ext[1:-1] - operate(widened, face_set, rate)[1:-1]
        update = residual / theta
        moved = current + update[1:-1]
        residual = residual[1:-1] - operate(update, inner_set, rate)[1:-1]
        update = update[1:-1]
        update = rho_two * rho_one * update + 2.0 * rho_two / delta * residual
        return moved + update

    bound_row = []
    starting = initial[0] * opened
    current = starting
    for fine_step in range(FINE):
        local = jnp.max(1.0 + 2.0 * conduct_sum + rates[fine_step] * speed_sum)
        bound_row.append(lax.pmax(local, "space"))
        current = advance(current, fine_step, bound_row[fine_step])
    advanced = current
    incoming = shifted(advanced, "tm", 1)
    current = jnp.where(lax.axis_index("tm") == 0, starting, incoming)
    for fine_step in range(FINE - 1):
        current = advance(current, fine_step, bound_row[fine_step])
    return (advanced[None], current[None])


def solution(mesh):
    in_specs = (
        P(("copy", "tm"), "space", None, None),
        P(("copy", "tm"), "space", None, None),
        P("space", None, None),
        P(None, "space", None, None),
        P("space", None, None),
        P("tm", None),
    )
    out_specs = (P(("copy", "tm"), "space", None, None), P(("copy", "tm"), "space", None, None))
    return jax.shard_map(shards, mesh=mesh, in_specs=in_specs, out_specs=out_specs, check_vma=False)
```

profile of v0, /device:TPU:0, one launch (start us, length us, event | category | flops | bytes accessed | tf_op | source)
XLA Modules:
  0.0 163.1 jit_solution(1393754445144058209)
XLA Ops:
  0.6 1.1 multiply_bitcast_fusion
  1.8 1.1 pad_maximum_fusion.1
  2.9 4.9 %collective-permute-start.2 = (f32[5,2,128,128]{3,2,1,0:T(8,128)S(1)}, f32[5,2,128,128]{3,2,1,0:T(8,128)S(1)}, u32[]{:S(2)}, u32[]{:S(2)}) collective-permute-start(f32[5,2,128,128]{3,2,1,0:T(8,128)S(1)} %pad_maximum_fusion.1), channel_id=1, source_target_pairs={{0,1},{1,2},{2,3},{3,4},{4,5},{5,6},{6,7},{8,9},{9,10},{10,11},{11... | collective-permute-start | bytes 1966088 | tf_op jit(solution)/shard_map/ppermute | solution.py:17
  7.8 1.3 collective-permute-start.3
  9.1 4.6 %collective-permute-start = (f32[2,128,128]{2,1,0:T(8,128)S(1)}, f32[2,128,128]{2,1,0:T(8,128)S(1)}, u32[]{:S(2)}, u32[]{:S(2)}) collective-permute-start(f32[2,128,128]{2,1,0:T(8,128)S(1)} %get-tuple-element.89), channel_id=1, source_target_pairs={{0,1},{1,2},{2,3},{3,4},{4,5},{5,6},{6,7},{8,9},{9,10},{10,11},{11... | collective-permute-start | bytes 393224 | tf_op jit(solution)/shard_map/ppermute | solution.py:17
  13.7 1.3 collective-permute-start.1
  15.0 0.6 fusion.110
  15.6 25.8 %collective-permute-done = f32[2,128,128]{2,1,0:T(8,128)S(1)} collective-permute-done((f32[2,128,128]{2,1,0:T(8,128)S(1)}, f32[2,128,128]{2,1,0:T(8,128)S(1)}, u32[]{:S(2)}, u32[]{:S(2)}) %collective-permute-start) | collective-permute-done | bytes 131104 | tf_op jit(solution)/shard_map/ppermute | solution.py:17
  41.9 0.3 copy-done
  42.2 0.4 copy-done.3
  43.6 0.2 fusion.106
  43.8 0.7 slice-done
  44.5 2.1 %fusion.1 = (f32[6,128,128]{2,1,0:T(8,128)}, f32[6,128,128]{2,1,0:T(8,128)S(1)}, f32[6,128,128]{2,1,0:T(8,128)}, f32[6,128,128]{2,1,0:T(8,128)S(1)}, f32[6,128,128]{2,1,0:T(8,128)S(1)}, /*index=5*/f32[6,128,128]{2,1,0:T(8,128)S(1)}) fusion(f32[5,128,128]{2,1,0:T(8,128)S(1)} %slice-done, f32[6,128,128]{2,1,0:T(8,128)S(1)} %get-tuple-element.26, f32[]{:T(128)} %bitcast.7, ...), kind=kLoop, calls=%fused_computation.17 | loop fusion | flops 2850816 | bytes 6541316 | tf_op jit(solution)/shard_map/add | solution.py:76
  46.6 1.6 %multiply_add_fusion.12 = (f32[6,128,128]{2,1,0:T(8,128)}, f32[6,128,128]{2,1,0:T(8,128)S(1)}) fusion(f32[6,128,127]{2,1,0:T(8,128)S(1)} %slice.663, f32[6,128,128]{2,1,0:T(8,128)S(1)} %get-tuple-element.40, f32[]{:T(128)} %bitcast.7, f32[2,128,128]{2,1,0:T(8,128)S(1)} %collective-permute-done.1, f32[2,128,128]{2,1,0:T(8,128)S(1)} %get-tuple-element.89, ...), kind=kLoop, calls=%fused_computation.71 | loop fusion | flops 1179648 | bytes 2746372 | tf_op jit(solution)/shard_map/add | solution.py:76
  48.3 3.5 %add_reduce_fusion = (f32[]{:T(128)}, f32[]{:T(128)}, f32[]{:T(128)}, f32[]{:T(128)}) fusion(f32[]{:T(128)} %bitcast.14, f32[]{:T(128)} %bitcast.13, f32[]{:T(128)} %bitcast.12, f32[]{:T(128)} %bitcast.7, f32[6,128,127]{2,1,0:T(8,128)S(1)} %bitcast.98, f32[6,128,128]{2,1,0:T(8,128)S(1)} %get-tuple-element.36, f32[6,127,128]{2,1,0:T(8,128)S(1)} %bitcast.99, ...), kind=kLoop, calls=%fused_computation.280 | loop fusion | flops 786428 | bytes 3002400 | tf_op jit(solution)/shard_map/reduce_max | solution.py:123
  51.7 22.3 %all-reduce.99 = (f32[]{:T(128)}, f32[]{:T(128)}, f32[]{:T(128)}, f32[]{:T(128)}) all-reduce(f32[]{:T(128)} %get-tuple-element.5, f32[]{:T(128)} %get-tuple-element.4, f32[]{:T(128)} %get-tuple-element.3, f32[]{:T(128)} %get-tuple-element.2), channel_id=1, replica_groups=mesh['copy'=2,'tm'=2,'space'=8] {'space'}, use_global_device_ids=true, to_apply=%region_1.2 | all-reduce | flops 4 | bytes 32 | tf_op jit(solution)/shard_map/pmax | solution.py:124
  75.5 1.0 slice.655
  76.5 2.2 %broadcast_divide_fusion.6 = (f32[4,128,128]{2,1,0:T(8,128)S(1)}, f32[4,128,128]{2,1,0:T(8,128)}, f32[4,128,128]{2,1,0:T(8,128)S(1)}) fusion(f32[]{:T(128)S(6)} %mul.815, f32[6,128,127]{2,1,0:T(8,128)} %bitcast.100, f32[6,128,128]{2,1,0:T(8,128)} %get-tuple-element.35, f32[6,127,128]{2,1,0:T(8,128)} %bitcast.101, f32[6,128,128]{2,1,0:T(8,128)} %get-tuple-element.37, ...), kind=kLoop, calls=%fused_computation.288 | loop fusion | flops 851968 | bytes 4909060 | tf_op jit(solution)/shard_map/div | solution.py:112
  78.7 0.7 slice.691
  79.5 0.8 slice.695
  80.3 0.7 slice.687
  81.0 2.0 %fusion.33 = (f32[4,128,128]{2,1,0:T(8,128)S(1)}, f32[4,128,128]{2,1,0:T(8,128)S(1)}, f32[4,128,128]{2,1,0:T(8,128)S(1)}) fusion(f32[4,128,128]{2,1,0:T(8,128)S(1)} %get-tuple-element.22, f32[3,128,128]{2,1,0:T(8,128)} %slice.687, f32[6,128,128]{2,1,0:T(8,128)S(1)} %get-tuple-element.32, f32[]{:T(128)} %bitcast.7, f32[6,128,128]{2,1,0:T(8,128)S(1)} %get-tuple-element.26, ...), kind=kLoop, calls=%fused_computation.96 | loop fusion | flops 1769472 | bytes 3338244 | tf_op jit(solution)/shard_map/add | solution.py:76
  83.3 1.7 %collective-permute-start.4 = (f32[2,128,128]{2,1,0:T(8,128)S(1)}, f32[2,128,128]{2,1,0:T(8,128)S(1)}, u32[]{:S(2)}, u32[]{:S(2)}) collective-permute-start(f32[2,128,128]{2,1,0:T(8,128)S(1)} %fusion.95), channel_id=1, source_target_pairs={{0,1},{1,2},{2,3},{3,4},{4,5},{5,6},{6,7},{8,9},{9,10},{10,11},{11... | collective-permute-start | bytes 393224 | tf_op jit(solution)/shard_map/ppermute | solution.py:17
  85.0 1.3 collective-permute-start.5
  87.6 4.2 %collective-permute-done.5 = f32[2,128,128]{2,1,0:T(8,128)S(1)} collective-permute-done((f32[2,128,128]{2,1,0:T(8,128)S(1)}, f32[2,128,128]{2,1,0:T(8,128)S(1)}, u32[]{:S(2)}, u32[]{:S(2)}) %collective-permute-start.5) | collective-permute-done | bytes 131104 | tf_op jit(solution)/shard_map/ppermute | solution.py:20
  92.1 1.0 fusion.5
  93.1 0.2 broadcast_divide_fusion.4
  93.5 0.9 fusion.37
  94.6 3.3 %collective-permute-start.6 = (f32[2,128,128]{2,1,0:T(8,128)S(1)}, f32[2,128,128]{2,1,0:T(8,128)S(1)}, u32[]{:S(2)}, u32[]{:S(2)}) collective-permute-start(f32[2,128,128]{2,1,0:T(8,128)S(1)} %fusion.91), channel_id=1, source_target_pairs={{0,1},{1,2},{2,3},{3,4},{4,5},{5,6},{6,7},{8,9},{9,10},{10,11},{11... | collective-permute-start | bytes 393224 | tf_op jit(solution)/shard_map/ppermute | solution.py:17
  97.9 1.3 collective-permute-start.7
  100.7 4.0 %collective-permute-done.7 = f32[2,128,128]{2,1,0:T(8,128)S(1)} collective-permute-done((f32[2,128,128]{2,1,0:T(8,128)S(1)}, f32[2,128,128]{2,1,0:T(8,128)S(1)}, u32[]{:S(2)}, u32[]{:S(2)}) %collective-permute-start.7) | collective-permute-done | bytes 131104 | tf_op jit(solution)/shard_map/ppermute | solution.py:20
  105.0 1.0 fusion.9
  106.0 0.2 broadcast_divide_fusion.2
  106.4 0.9 fusion.41
  107.5 2.8 %collective-permute-start.8 = (f32[2,128,128]{2,1,0:T(8,128)S(1)}, f32[2,128,128]{2,1,0:T(8,128)S(1)}, u32[]{:S(2)}, u32[]{:S(2)}) collective-permute-start(f32[2,128,128]{2,1,0:T(8,128)S(1)} %fusion.87), channel_id=1, source_target_pairs={{0,1},{1,2},{2,3},{3,4},{4,5},{5,6},{6,7},{8,9},{9,10},{10,11},{11... | collective-permute-start | bytes 393224 | tf_op jit(solution)/shard_map/ppermute | solution.py:17
  110.3 1.3 collective-permute-start.9
  112.9 4.3 %collective-permute-done.9 = f32[2,128,128]{2,1,0:T(8,128)S(1)} collective-permute-done((f32[2,128,128]{2,1,0:T(8,128)S(1)}, f32[2,128,128]{2,1,0:T(8,128)S(1)}, u32[]{:S(2)}, u32[]{:S(2)}) %collective-permute-start.9) | collective-permute-done | bytes 131104 | tf_op jit(solution)/shard_map/ppermute | solution.py:20
  117.5 1.0 fusion.13
  118.5 0.2 broadcast_divide_fusion
  118.9 0.9 fusion.45
  120.0 1.3 collective-permute-start.10
  121.3 1.0 collective-permute-done.10
  122.3 2.8 %collective-permute-start.11 = (f32[2,128,128]{2,1,0:T(8,128)S(1)}, f32[2,128,128]{2,1,0:T(8,128)S(1)}, u32[]{:S(2)}, u32[]{:S(2)}) collective-permute-start(f32[2,128,128]{2,1,0:T(8,128)S(1)} %broadcast_select_fusion), channel_id=1, source_target_pairs={{0,1},{1,2},{2,3},{3,4},{4,5},{5,6},{6,7},{8,9},{9,10},{10,11},{11... | collective-permute-start | bytes 393224 | tf_op jit(solution)/shard_map/ppermute | solution.py:17
  125.2 1.3 collective-permute-start.12
  126.5 1.9 %collective-permute-done.11 = f32[2,128,128]{2,1,0:T(8,128)S(1)} collective-permute-done((f32[2,128,128]{2,1,0:T(8,128)S(1)}, f32[2,128,128]{2,1,0:T(8,128)S(1)}, u32[]{:S(2)}, u32[]{:S(2)}) %collective-permute-start.11) | collective-permute-done | bytes 131104 | tf_op jit(solution)/shard_map/ppermute | solution.py:17
  128.4 4.1 %collective-permute-done.12 = f32[2,128,128]{2,1,0:T(8,128)S(1)} collective-permute-done((f32[2,128,128]{2,1,0:T(8,128)S(1)}, f32[2,128,128]{2,1,0:T(8,128)S(1)}, u32[]{:S(2)}, u32[]{:S(2)}) %collective-permute-start.12) | collective-permute-done | bytes 131104 | tf_op jit(solution)/shard_map/ppermute | solution.py:20
  132.8 1.0 fusion.17
  133.9 0.2 broadcast_divide_fusion.5
  134.3 0.9 fusion.49
  135.3 3.3 %collective-permute-start.13 = (f32[2,128,128]{2,1,0:T(8,128)S(1)}, f32[2,128,128]{2,1,0:T(8,128)S(1)}, u32[]{:S(2)}, u32[]{:S(2)}) collective-permute-start(f32[2,128,128]{2,1,0:T(8,128)S(1)} %fusion.79), channel_id=1, source_target_pairs={{0,1},{1,2},{2,3},{3,4},{4,5},{5,6},{6,7},{8,9},{9,10},{10,11},{11... | collective-permute-start | bytes 393224 | tf_op jit(solution)/shard_map/ppermute | solution.py:17
  138.6 1.3 collective-permute-start.14
  139.9 1.2 collective-permute-done.13
  141.1 4.4 %collective-permute-done.14 = f32[2,128,128]{2,1,0:T(8,128)S(1)} collective-permute-done((f32[2,128,128]{2,1,0:T(8,128)S(1)}, f32[2,128,128]{2,1,0:T(8,128)S(1)}, u32[]{:S(2)}, u32[]{:S(2)}) %collective-permute-start.14) | collective-permute-done | bytes 131104 | tf_op jit(solution)/shard_map/ppermute | solution.py:20
  145.8 1.0 fusion.21
  146.8 0.2 broadcast_divide_fusion.3
  147.2 0.9 fusion.53
  148.3 4.5 %collective-permute-start.15 = (f32[2,128,128]{2,1,0:T(8,128)S(1)}, f32[2,128,128]{2,1,0:T(8,128)S(1)}, u32[]{:S(2)}, u32[]{:S(2)}) collective-permute-start(f32[2,128,128]{2,1,0:T(8,128)S(1)} %fusion.75), channel_id=1, source_target_pairs={{0,1},{1,2},{2,3},{3,4},{4,5},{5,6},{6,7},{8,9},{9,10},{10,11},{11... | collective-permute-start | bytes 393224 | tf_op jit(solution)/shard_map/ppermute | solution.py:17
  152.8 1.3 collective-permute-start.16
  154.1 1.3 collective-permute-done.15
  155.4 4.3 %collective-permute-done.16 = f32[2,128,128]{2,1,0:T(8,128)S(1)} collective-permute-done((f32[2,128,128]{2,1,0:T(8,128)S(1)}, f32[2,128,128]{2,1,0:T(8,128)S(1)}, u32[]{:S(2)}, u32[]{:S(2)}) %collective-permute-start.16) | collective-permute-done | bytes 131104 | tf_op jit(solution)/shard_map/ppermute | solution.py:20
  160.0 1.0 fusion.25
  161.0 0.2 broadcast_divide_fusion.1
  161.4 0.9 fusion.57
  162.3 0.8 fusion.71
  (101 shorter events, 4.8 us)
Async XLA Ops:
  0.6 14.3 %copy-start.8 = (f32[1,4]{1,0:T(1,128)S(1)}, f32[1,4]{1,0:T(1,128)}, u32[]{:S(2)}) copy-start(f32[1,4]{1,0:T(1,128)} %param.11) | copy-start | bytes 52
  1.7 39.9 %copy-start.5 = (f32[1,2,128,128]{3,2,1,0:T(8,128)}, f32[1,2,128,128]{3,2,1,0:T(8,128)S(1)}, u32[]{:S(2)}) copy-start(f32[1,2,128,128]{3,2,1,0:T(8,128)S(1)} %get-tuple-element.88) | copy-start | bytes 393220
  1.8 39.9 %copy-start.2 = (f32[3,2,128,128]{3,2,1,0:T(8,128)S(1)}, f32[3,2,128,128]{3,2,1,0:T(8,128)}, u32[]{:S(2)}) copy-start(f32[3,2,128,128]{3,2,1,0:T(8,128)} %param.9) | copy-start | bytes 1179652
  2.9 38.8 %collective-permute-start.2 = (f32[5,2,128,128]{3,2,1,0:T(8,128)S(1)}, f32[5,2,128,128]{3,2,1,0:T(8,128)S(1)}, u32[]{:S(2)}, u32[]{:S(2)}) collective-permute-start(f32[5,2,128,128]{3,2,1,0:T(8,128)S(1)} %pad_maximum_fusion.1), channel_id=1, source_target_pairs={{0,1},{1,2},{2,3},{3,4},{4,5},{5,6},{6,7},{8,9},{9,10},{10,11},{11... | collective-permute-start | bytes 1966088 | tf_op jit(solution)/shard_map/ppermute | solution.py:17
  7.8 33.9 %collective-permute-start.3 = (f32[5,2,128,128]{3,2,1,0:T(8,128)S(1)}, f32[5,2,128,128]{3,2,1,0:T(8,128)S(1)}, u32[]{:S(2)}, u32[]{:S(2)}) collective-permute-start(f32[5,2,128,128]{3,2,1,0:T(8,128)S(1)} %pad_maximum_fusion.1), channel_id=1, source_target_pairs={{1,0},{2,1},{3,2},{4,3},{5,4},{6,5},{7,6},{9,8},{10,9},{11,10},{12... | collective-permute-start | bytes 1966088 | tf_op jit(solution)/shard_map/ppermute | solution.py:20
  9.1 32.3 %collective-permute-start = (f32[2,128,128]{2,1,0:T(8,128)S(1)}, f32[2,128,128]{2,1,0:T(8,128)S(1)}, u32[]{:S(2)}, u32[]{:S(2)}) collective-permute-start(f32[2,128,128]{2,1,0:T(8,128)S(1)} %get-tuple-element.89), channel_id=1, source_target_pairs={{0,1},{1,2},{2,3},{3,4},{4,5},{5,6},{6,7},{8,9},{9,10},{10,11},{11... | collective-permute-start | bytes 393224 | tf_op jit(solution)/shard_map/ppermute | solution.py:17
  13.7 27.7 %collective-permute-start.1 = (f32[2,128,128]{2,1,0:T(8,128)S(1)}, f32[2,128,128]{2,1,0:T(8,128)S(1)}, u32[]{:S(2)}, u32[]{:S(2)}) collective-permute-start(f32[2,128,128]{2,1,0:T(8,128)S(1)} %get-tuple-element.89), channel_id=1, source_target_pairs={{1,0},{2,1},{3,2},{4,3},{5,4},{6,5},{7,6},{9,8},{10,9},{11,10},{12... | collective-permute-start | bytes 393224 | tf_op jit(solution)/shard_map/ppermute | solution.py:20
  41.4 0.7 copy-start
  41.6 0.9 copy-start.3
  41.7 1.0 copy-start.4
  43.5 1.0 slice-start
  48.3 28.2 %copy-start.1 = (f32[6,128,128]{2,1,0:T(8,128)S(1)}, f32[6,128,128]{2,1,0:T(8,128)}, u32[]{:S(2)}) copy-start(f32[6,128,128]{2,1,0:T(8,128)} %copy-done) | copy-start | bytes 1179652
  81.0 2.1 %copy-start.6 = (f32[4,128,128]{2,1,0:T(8,128)S(1)}, f32[4,128,128]{2,1,0:T(8,128)}, u32[]{:S(2)}) copy-start(f32[4,128,128]{2,1,0:T(8,128)} %get-tuple-element.23) | copy-start | bytes 786436
  83.3 4.3 %collective-permute-start.4 = (f32[2,128,128]{2,1,0:T(8,128)S(1)}, f32[2,128,128]{2,1,0:T(8,128)S(1)}, u32[]{:S(2)}, u32[]{:S(2)}) collective-permute-start(f32[2,128,128]{2,1,0:T(8,128)S(1)} %fusion.95), channel_id=1, source_target_pairs={{0,1},{1,2},{2,3},{3,4},{4,5},{5,6},{6,7},{8,9},{9,10},{10,11},{11... | collective-permute-start | bytes 393224 | tf_op jit(solution)/shard_map/ppermute | solution.py:17
  85.0 6.9 %collective-permute-start.5 = (f32[2,128,128]{2,1,0:T(8,128)S(1)}, f32[2,128,128]{2,1,0:T(8,128)S(1)}, u32[]{:S(2)}, u32[]{:S(2)}) collective-permute-start(f32[2,128,128]{2,1,0:T(8,128)S(1)} %fusion.95), channel_id=1, source_target_pairs={{1,0},{2,1},{3,2},{4,3},{5,4},{6,5},{7,6},{9,8},{10,9},{11,10},{12... | collective-permute-start | bytes 393224 | tf_op jit(solution)/shard_map/ppermute | solution.py:20
  94.6 6.1 %collective-permute-start.6 = (f32[2,128,128]{2,1,0:T(8,128)S(1)}, f32[2,128,128]{2,1,0:T(8,128)S(1)}, u32[]{:S(2)}, u32[]{:S(2)}) collective-permute-start(f32[2,128,128]{2,1,0:T(8,128)S(1)} %fusion.91), channel_id=1, source_target_pairs={{0,1},{1,2},{2,3},{3,4},{4,5},{5,6},{6,7},{8,9},{9,10},{10,11},{11... | collective-permute-start | bytes 393224 | tf_op jit(solution)/shard_map/ppermute | solution.py:17
  97.9 6.9 %collective-permute-start.7 = (f32[2,128,128]{2,1,0:T(8,128)S(1)}, f32[2,128,128]{2,1,0:T(8,128)S(1)}, u32[]{:S(2)}, u32[]{:S(2)}) collective-permute-start(f32[2,128,128]{2,1,0:T(8,128)S(1)} %fusion.91), channel_id=1, source_target_pairs={{1,0},{2,1},{3,2},{4,3},{5,4},{6,5},{7,6},{9,8},{10,9},{11,10},{12... | collective-permute-start | bytes 393224 | tf_op jit(solution)/shard_map/ppermute | solution.py:20
  107.5 5.4 %collective-permute-start.8 = (f32[2,128,128]{2,1,0:T(8,128)S(1)}, f32[2,128,128]{2,1,0:T(8,128)S(1)}, u32[]{:S(2)}, u32[]{:S(2)}) collective-permute-start(f32[2,128,128]{2,1,0:T(8,128)S(1)} %fusion.87), channel_id=1, source_target_pairs={{0,1},{1,2},{2,3},{3,4},{4,5},{5,6},{6,7},{8,9},{9,10},{10,11},{11... | collective-permute-start | bytes 393224 | tf_op jit(solution)/shard_map/ppermute | solution.py:17
  110.3 6.9 %collective-permute-start.9 = (f32[2,128,128]{2,1,0:T(8,128)S(1)}, f32[2,128,128]{2,1,0:T(8,128)S(1)}, u32[]{:S(2)}, u32[]{:S(2)}) collective-permute-start(f32[2,128,128]{2,1,0:T(8,128)S(1)} %fusion.87), channel_id=1, source_target_pairs={{1,0},{2,1},{3,2},{4,3},{5,4},{6,5},{7,6},{9,8},{10,9},{11,10},{12... | collective-permute-start | bytes 393224 | tf_op jit(solution)/shard_map/ppermute | solution.py:20
  120.0 13.8 %copy-start.7 = (f32[2,128,128]{2,1,0:T(8,128)}, f32[2,128,128]{2,1,0:T(8,128)S(1)}, u32[]{:S(2)}) copy-start(f32[2,128,128]{2,1,0:T(8,128)S(1)} %fusion.83) | copy-start | bytes 393220
  120.0 2.3 %collective-permute-start.10 = (f32[2,128,128]{2,1,0:T(8,128)S(1)}, f32[2,128,128]{2,1,0:T(8,128)S(1)}, u32[]{:S(2)}, u32[]{:S(2)}) collective-permute-start(f32[2,128,128]{2,1,0:T(8,128)S(1)} %fusion.83), channel_id=1, source_target_pairs={{0,8},{1,9},{2,10},{3,11},{4,12},{5,13},{6,14},{7,15},{16,24},{17,... | collective-permute-start | bytes 393224 | tf_op jit(solution)/shard_map/ppermute | solution.py:28
  122.3 6.1 %collective-permute-start.11 = (f32[2,128,128]{2,1,0:T(8,128)S(1)}, f32[2,128,128]{2,1,0:T(8,128)S(1)}, u32[]{:S(2)}, u32[]{:S(2)}) collective-permute-start(f32[2,128,128]{2,1,0:T(8,128)S(1)} %broadcast_select_fusion), channel_id=1, source_target_pairs={{0,1},{1,2},{2,3},{3,4},{4,5},{5,6},{6,7},{8,9},{9,10},{10,11},{11... | collective-permute-start | bytes 393224 | tf_op jit(solution)/shard_map/ppermute | solution.py:17
  125.2 7.4 %collective-permute-start.12 = (f32[2,128,128]{2,1,0:T(8,128)S(1)}, f32[2,128,128]{2,1,0:T(8,128)S(1)}, u32[]{:S(2)}, u32[]{:S(2)}) collective-permute-start(f32[2,128,128]{2,1,0:T(8,128)S(1)} %broadcast_select_fusion), channel_id=1, source_target_pairs={{1,0},{2,1},{3,2},{4,3},{5,4},{6,5},{7,6},{9,8},{10,9},{11,10},{12... | collective-permute-start | bytes 393224 | tf_op jit(solution)/shard_map/ppermute | solution.py:20
  135.3 5.8 %collective-permute-start.13 = (f32[2,128,128]{2,1,0:T(8,128)S(1)}, f32[2,128,128]{2,1,0:T(8,128)S(1)}, u32[]{:S(2)}, u32[]{:S(2)}) collective-permute-start(f32[2,128,128]{2,1,0:T(8,128)S(1)} %fusion.79), channel_id=1, source_target_pairs={{0,1},{1,2},{2,3},{3,4},{4,5},{5,6},{6,7},{8,9},{9,10},{10,11},{11... | collective-permute-start | bytes 393224 | tf_op jit(solution)/shard_map/ppermute | solution.py:17
  138.6 6.9 %collective-permute-start.14 = (f32[2,128,128]{2,1,0:T(8,128)S(1)}, f32[2,128,128]{2,1,0:T(8,128)S(1)}, u32[]{:S(2)}, u32[]{:S(2)}) collective-permute-start(f32[2,128,128]{2,1,0:T(8,128)S(1)} %fusion.79), channel_id=1, source_target_pairs={{1,0},{2,1},{3,2},{4,3},{5,4},{6,5},{7,6},{9,8},{10,9},{11,10},{12... | collective-permute-start | bytes 393224 | tf_op jit(solution)/shard_map/ppermute | solution.py:20
  148.3 7.1 %collective-permute-start.15 = (f32[2,128,128]{2,1,0:T(8,128)S(1)}, f32[2,128,128]{2,1,0:T(8,128)S(1)}, u32[]{:S(2)}, u32[]{:S(2)}) collective-permute-start(f32[2,128,128]{2,1,0:T(8,128)S(1)} %fusion.75), channel_id=1, source_target_pairs={{0,1},{1,2},{2,3},{3,4},{4,5},{5,6},{6,7},{8,9},{9,10},{10,11},{11... | collective-permute-start | bytes 393224 | tf_op jit(solution)/shard_map/ppermute | solution.py:17
  152.8 6.9 %collective-permute-start.16 = (f32[2,128,128]{2,1,0:T(8,128)S(1)}, f32[2,128,128]{2,1,0:T(8,128)S(1)}, u32[]{:S(2)}, u32[]{:S(2)}) collective-permute-start(f32[2,128,128]{2,1,0:T(8,128)S(1)} %fusion.75), channel_id=1, source_target_pairs={{1,0},{2,1},{3,2},{4,3},{5,4},{6,5},{7,6},{9,8},{10,9},{11,10},{12... | collective-permute-start | bytes 393224 | tf_op jit(solution)/shard_map/ppermute | solution.py:20
where the time goes:
time: 164 us; the launch traced here: 163 us
  waiting for transfers between devices  56.4 us (34%)
  starting transfers between devices  39.5 us (24%)
  other arithmetic  28.7 us (18%)
  blocking collectives  22.3 us (14%)
  local copies, waits for them, and re-layouts  8.9 us (5%)
  between operations  7.29 us (4%)
    ppermute x8, waiting for transfers between devices, extended(): lax.ppermute(lax.slice_in_dim(block, block.shape[dim] - width, None, axis...  30.2 us
    ppermute x8, starting transfers between devices, extended(): lax.ppermute(lax.slice_in_dim(block, block.shape[dim] - width, None, axis...  27.9 us
    ppermute x8, waiting for transfers between devices, extended(): lax.ppermute(lax.slice_in_dim(block, 0, width, axis=dim), axis, backward)  25.3 us
    pmax x1, blocking collectives, shards(): bound_row.append(lax.pmax(local, 'space'))  22.3 us
    add x15, other arithmetic, operate(): conduct * (values - neighbor)  17.3 us
    ppermute x8, starting transfers between devices, extended(): lax.ppermute(lax.slice_in_dim(block, 0, width, axis=dim), axis, backward)  10.3 us
    slice x51, local copies, waits for them, and re-layouts, ahead(): tail = lax.slice_in_dim(values, 1, length, axis=direction)  6.02 us
    div x7, other arithmetic, advance(): update = residual / theta  3.55 us
  transfers between devices with their start and end apart: 17, of which 11 were waited for; matrix products, arithmetic and copies ran while one was open for 1% of the time, Pallas kernels for 0%

commit v1 on v0

v1 whole, which is shorter than its diff:
```python
import functools

import jax
import jax.numpy as jnp
from jax import lax
from jax.experimental import pallas as pl
from jax.experimental.pallas import tpu as pltpu
from jax.sharding import PartitionSpec as P

LOWER = 0.5
MESH = pl.DeviceIdType.MESH


def place(index, count):
    if count % 4:
        return index
    return index + ((index // 2) % 2) * (1 - 2 * (index % 2))


def drain(view, sem):
    pltpu.make_async_copy(view, view, sem).wait()


def after(values, axis):
    length = values.shape[axis]
    return pltpu.roll(values, length - 1, axis)


def before(values, axis):
    return pltpu.roll(values, 1, axis)


def kernel(
    slabs, blocks, rows, width, per, groups,
    initial_ref, source_ref, diffusion_ref, wind_ref, buildings_ref, strength_ref,
    advanced_ref, final_ref,
    initial, source, diffusion, wind, buildings,
    sendc, sends, recvc, recvs, raw, states, rates, gath, outs, back,
    load_sem, a2a_sem, rate_sem, gath_sem, halo_send, halo_recv, out_sem,
):
    layers, ny, nz = diffusion.shape
    nx = slabs * layers
    cores = slabs * blocks
    fine = strength_ref.shape[1]
    ext = rows + 2 * width
    space = lax.axis_index("space")
    time = lax.axis_index("tm")
    mine = place(space, slabs) * blocks + time

    def where(core):
        return {"space": place(core // blocks, slabs), "tm": core % blocks}

    loads = [
        pltpu.make_async_copy(a, b, load_sem.at[i])
        for i, (a, b) in enumerate(
            (
                (buildings_ref, buildings),
                (diffusion_ref, diffusion),
                (wind_ref, wind),
                (initial_ref, initial),
                (source_ref, source),
            )
        )
    ]
    for load in loads:
        load.start()
    blank = jnp.zeros((width, nx, nz), jnp.float32)
    for field in range(raw.shape[0]):
        raw[field, 0:width] = blank
        raw[field, width + rows : ext] = blank
    for index in range(states.shape[0]):
        for block in range(blocks):
            states[index, block, 0:width] = blank
            states[index, block, width + rows : ext] = blank
    for k in range(fine):
        rates[time, k] = jnp.full((8, nz), strength_ref[0, k], jnp.float32)

    barrier = pltpu.get_barrier_semaphore()

    def greet(step, _):
        pl.semaphore_signal(barrier, inc=1, device_id=where((mine + step) % cores), device_id_type=MESH)
        return 0

    lax.fori_loop(1, cores, greet, 0)

    def pack(dest, field, array):
        for layer in range(layers):
            if rows % 8 == 0:
                dest[:, field, layer] = array[layer].reshape(cores, rows, nz)
            else:
                for core in range(cores):
                    dest[core, field, layer] = array[layer, core * rows : (core + 1) * rows]

    for load in loads:
        load.wait()
    opened = (1 - buildings[...]).astype(jnp.float32)
    pack(sendc, 0, diffusion[...] * opened)
    for axis in range(3):
        pack(sendc, 1 + axis, wind[axis])
    pack(sends, 0, initial[0] * opened)
    pack(sends, 1, source[0].astype(jnp.float32) * opened)
    pl.semaphore_wait(barrier, cores - 1)

    rate_copy = [
        pltpu.make_async_remote_copy(
            rates.at[time], rates.at[time], rate_sem.at[0], rate_sem.at[1],
            device_id={"tm": (time + 1) % blocks}, device_id_type=MESH,
        )
    ]
    rate_copy[0].start()

    def send_coef(step, _):
        target = (space + step) % slabs
        core = place(target, slabs) * blocks + time
        pltpu.make_async_remote_copy(
            sendc.at[core], recvc.at[space], a2a_sem.at[0], a2a_sem.at[1],
            device_id={"space": target}, device_id_type=MESH,
        ).start()
        return 0

    def send_state(step, _):
        core = (mine + step) % cores
        pltpu.make_async_remote_copy(
            sends.at[core], recvs.at[space * blocks + time], a2a_sem.at[2], a2a_sem.at[3],
            device_id=where(core), device_id_type=MESH,
        ).start()
        return 0

    lax.fori_loop(1, slabs, send_coef, 0)
    lax.fori_loop(1, cores, send_state, 0)
    pltpu.make_async_copy(sendc.at[mine], recvc.at[space], a2a_sem.at[1]).start()
    pltpu.make_async_copy(sends.at[mine], recvs.at[space * blocks + time], a2a_sem.at[3]).start()
    drain(recvc, a2a_sem.at[1])
    drain(recvs, a2a_sem.at[3])

    def turned(array):
        return jnp.swapaxes(array.reshape(nx, rows, nz), 0, 1)

    inside = slice(width, width + rows)
    for field in range(4):
        raw[field, inside] = turned(recvc[:, field])
    for block in range(blocks):
        for kind in range(2):
            chunk = jnp.stack([recvs[s * blocks + block, kind] for s in range(slabs)])
            raw[4 + kind * blocks + block, inside] = turned(chunk)

    last = cores - 1

    def swap(index, up_source, up_target, down_source, down_target):
        @pl.when(mine < last)
        def _():
            pltpu.make_async_remote_copy(
                up_source, up_target, halo_send.at[index, 0], halo_recv.at[index, 0],
                device_id=where(mine + 1), device_id_type=MESH,
            ).start()

        @pl.when(mine > 0)
        def _():
            pltpu.make_async_remote_copy(
                down_source, down_target, halo_send.at[index, 1], halo_recv.at[index, 1],
                device_id=where(mine - 1), device_id_type=MESH,
            ).start()

    def arrived(index, low, high):
        @pl.when(mine > 0)
        def _():
            drain(low, halo_recv.at[index, 0])

        @pl.when(mine < last)
        def _():
            drain(high, halo_recv.at[index, 1])

    def sent(index, low, high):
        @pl.when(mine < last)
        def _():
            drain(low, halo_send.at[index, 0])

        @pl.when(mine > 0)
        def _():
            drain(high, halo_send.at[index, 1])

    def views(ref):
        return (
            ref.at[:, rows : rows + width],
            ref.at[:, 0:width],
            ref.at[:, width : 2 * width],
            ref.at[:, width + rows : ext],
        )

    swap(0, *views(raw))
    raw_views = views(raw)
    arrived(0, raw_views[1], raw_views[3])
    for copy in rate_copy:
        copy.wait()

    masked = raw[0]
    core_open = jnp.where(masked > 0.0, 1.0, 0.0)
    level = lax.broadcasted_iota(jnp.int32, (ext, nx, nz), 1)
    lane = lax.broadcasted_iota(jnp.int32, (ext, nx, nz), 2)
    wind_x, wind_y, wind_z = raw[1], raw[2], raw[3]

    def face(cut, wind_here, wind_next, masked_next, open_next, masked_here, open_here):
        conduct = jnp.sqrt(masked_here * masked_next)
        velocity = 0.5 * (wind_here + wind_next) * open_here * open_next
        if cut is not None:
            conduct = jnp.where(cut, conduct, 0.0)
            velocity = jnp.where(cut, velocity, 0.0)
        return conduct, velocity

    conduct_x, speed_x = face(
        level < nx - 1, wind_x, after(wind_x, 1), after(masked, 1), after(core_open, 1), masked, core_open
    )
    conduct_z, speed_z = face(
        lane < nz - 1, wind_z, after(wind_z, 2), after(masked, 2), after(core_open, 2), masked, core_open
    )
    conduct_y, speed_y = face(
        None, wind_y[:-1], wind_y[1:], masked[1:], core_open[1:], masked[:-1], core_open[:-1]
    )
    mid = slice(1, ext - 1)
    parts = []
    for conduct, speed, axis in ((conduct_x, speed_x, 1), (conduct_z, speed_z, 2)):
        plus = jnp.maximum(speed, 0.0)
        minus = jnp.maximum(-speed, 0.0)
        parts.append(
            (conduct[mid], minus[mid], before(conduct, axis)[mid], before(plus, axis)[mid],
             plus[mid], before(minus, axis)[mid])
        )
    plus = jnp.maximum(speed_y, 0.0)
    minus = jnp.maximum(-speed_y, 0.0)
    parts.append((conduct_y[1:], minus[1:], conduct_y[:-1], plus[:-1], plus[1:], minus[:-1]))
    conduct_sum = sum(p[0] + p[2] for p in parts)
    flow_sum = sum(p[4] + p[5] for p in parts)
    speed_sum = sum(p[1] + p[3] for p in parts) + flow_sum

    own = slice(width - 1, width - 1 + rows)
    for block in range(blocks):
        for k in range(fine):
            rate = rates[block, k, 0:1]
            bound = 1.0 + 2.0 * conduct_sum[own] + rate * speed_sum[own]
            bound = jnp.max(jnp.max(bound, axis=0), axis=0, keepdims=True)
            j = block * fine + k
            gath[mine, j : j + 1] = bound

    def send_bound(step, _):
        pltpu.make_async_remote_copy(
            gath.at[mine], gath.at[mine], gath_sem.at[0], gath_sem.at[1],
            device_id=where((mine + step) % cores), device_id_type=MESH,
        ).start()
        return 0

    lax.fori_loop(1, cores, send_bound, 0)

    def stencil(values, faces, axis_shift):
        inner = values[1:-1]
        first, second, third = faces
        total = first[0] * after(inner, 1) + first[1] * before(inner, 1)
        total = total + second[0] * after(inner, 2) + second[1] * before(inner, 2)
        return total + third[0] * values[2:] + third[1] * values[:-2]

    weights = []

    def weight_rows():
        if not weights:
            drain(gath.at[0 : cores - 1], gath_sem.at[1])
            bound = jnp.max(jnp.max(gath[...], axis=0), axis=1, keepdims=True)
            bound = jnp.broadcast_to(bound, (gath.shape[1], nz))
            theta = (bound + LOWER) * 0.5
            delta = (bound - LOWER) * 0.5
            sigma = theta / delta
            rho_one = 1.0 / sigma
            rho_two = 1.0 / (2.0 * sigma - rho_one)
            beta = 2.0 * rho_two / (delta * theta)
            weights.append((1.0 + rho_two * rho_one) / theta + 2.0 * rho_two / delta)
            weights.append(beta)
        return weights

    def advance(values, off, block, k):
        count = ext - 2 * off
        rate = rates[block, k, 0:1]
        reach = slice(off, off + count - 2)
        faces = [(p[0][reach] + rate * p[1][reach], p[2][reach] + rate * p[3][reach]) for p in parts]
        diagonal = conduct_sum[reach] + rate * flow_sum[reach]
        forcing = raw[4 + blocks + block, off + 1 : off + count - 1]
        residual = forcing - diagonal * values[1:-1] + stencil(values, faces, 0)
        narrow = [(a[1:-1], b[1:-1]) for a, b in faces]
        inner = residual[1:-1]
        applied = inner + diagonal[1:-1] * inner - stencil(residual, narrow, 0)
        alpha, beta = weight_rows()
        j = block * fine + k
        return values[2:-2] + alpha[j : j + 1] * inner - beta[j : j + 1] * applied

    def deliver(slot, owner_block, value):
        outs[slot] = jnp.swapaxes(value, 0, 1).reshape(slabs, layers, rows, nz)
        kind = slot // blocks

        def send(step, _):
            target = (space + step) % slabs
            pltpu.make_async_remote_copy(
                outs.at[slot, target], back.at[kind, mine], out_sem.at[slot], out_sem.at[2 * blocks + kind],
                device_id={"space": target, "tm": owner_block}, device_id_type=MESH,
            ).start()
            return 0

        lax.fori_loop(1, slabs, send, 0)

        @pl.when(time == owner_block)
        def _():
            pltpu.make_async_copy(
                outs.at[slot, space], back.at[kind, mine], out_sem.at[2 * blocks + kind]
            ).start()

        @pl.when(time != owner_block)
        def _():
            pltpu.make_async_remote_copy(
                outs.at[slot, space], back.at[kind, mine], out_sem.at[slot], out_sem.at[2 * blocks + kind],
                device_id={"tm": owner_block}, device_id_type=MESH,
            ).start()

    def settled(slot, owner_block):
        drain(outs.at[slot, 0 : slabs - 1], out_sem.at[slot])

        @pl.when(time != owner_block)
        def _():
            drain(outs.at[slot, 0], out_sem.at[slot])

    def trim(values, off):
        low = width - off
        return values[low : low + rows]

    exchange = 0
    current = [raw[4 + block] for block in range(blocks)]
    off = 0
    live = list(range(blocks))
    exchanges = []
    for step in range(2 * fine - 1):
        second = step >= fine
        k = step - fine if second else step
        if step == fine:
            live = [blocks - 1]
        if step and (off + 2 > width):
            for block in live:
                states[exchange, block, inside] = trim(current[block], off)
            part = states.at[exchange, live[0] : live[-1] + 1]
            cuts = (
                part.at[:, rows : rows + width], part.at[:, 0:width],
                part.at[:, width : 2 * width], part.at[:, width + rows : ext],
            )
            swap(exchange + 1, *cuts)
            arrived(exchange + 1, cuts[1], cuts[3])
            exchanges.append((exchange + 1, cuts))
            for block in live:
                current[block] = states[exchange, block]
            off = 0
            exchange += 1
        for block in live:
            current[block] = advance(current[block], off, block, k)
        off += 2
        if step == fine - 2:
            deliver(blocks, 0, trim(current[0], off))
        if step == fine - 1:
            for block in range(blocks):
                deliver(block, block, trim(current[block], off))
            current[1] = current[0]
    deliver(blocks + 1, 1, trim(current[1], off))

    def unpack(dest, kind):
        for layer in range(layers):
            if rows % 8 == 0:
                dest[0, layer] = back[kind, :, layer].reshape(ny, nz)
            else:
                for core in range(cores):
                    dest[0, layer, core * rows : (core + 1) * rows] = back[kind, core, layer]

    drain(back.at[0], out_sem.at[2 * blocks])
    unpack(advanced_ref, 0)
    sent(0, raw_views[0], raw_views[2])
    for index, cuts in exchanges:
        sent(index, cuts[0], cuts[2])
    drain(recvc.at[0 : slabs - 1], a2a_sem.at[0])
    drain(recvs.at[0 : cores - 1], a2a_sem.at[2])
    drain(gath.at[0 : cores - 1], gath_sem.at[0])
    for kind in range(2):
        for block in range(blocks):
            settled(kind * blocks + block, block)
    drain(back.at[1], out_sem.at[2 * blocks + 1])
    unpack(final_ref, 1)


def solution(mesh):
    slabs = mesh.shape["space"]
    blocks = mesh.shape["tm"]

    def shards(initial, source, diffusion, wind_field, buildings, strength):
        layers, ny, nz = diffusion.shape
        nx = layers * slabs
        cores = slabs * blocks
        rows = ny // cores
        fine = strength.shape[1]
        width = 4 if rows >= 4 else 2
        per = width // 2
        groups = -(-(2 * fine - 1) // per) - 1
        ext = rows + 2 * width
        f32 = jnp.float32
        return pl.pallas_call(
            functools.partial(kernel, slabs, blocks, rows, width, per, groups),
            out_shape=[jax.ShapeDtypeStruct(initial.shape, f32)] * 2,
            in_specs=[pl.BlockSpec(memory_space=pl.ANY)] * 5 + [pl.BlockSpec(memory_space=pltpu.SMEM)],
            out_specs=[pl.BlockSpec(memory_space=pltpu.VMEM)] * 2,
            scratch_shapes=[
                pltpu.VMEM(initial.shape, f32),
                pltpu.VMEM(source.shape, source.dtype),
                pltpu.VMEM(diffusion.shape, f32),
                pltpu.VMEM(wind_field.shape, f32),
                pltpu.VMEM(buildings.shape, buildings.dtype),
                pltpu.VMEM((cores, 4, layers, rows, nz), f32),
                pltpu.VMEM((cores, 2, layers, rows, nz), f32),
                pltpu.VMEM((slabs, 4, layers, rows, nz), f32),
                pltpu.VMEM((cores, 2, layers, rows, nz), f32),
                pltpu.VMEM((4 + 2 * blocks, ext, nx, nz), f32),
                pltpu.VMEM((groups, blocks, ext, nx, nz), f32),
                pltpu.VMEM((blocks, fine, 8, nz), f32),
                pltpu.VMEM((cores, blocks * fine, nz), f32),
                pltpu.VMEM((2 * blocks, slabs, layers, rows, nz), f32),
                pltpu.VMEM((2, cores, layers, rows, nz), f32),
                pltpu.SemaphoreType.DMA((5,)),
                pltpu.SemaphoreType.DMA((4,)),
                pltpu.SemaphoreType.DMA((2,)),
                pltpu.SemaphoreType.DMA((2,)),
                pltpu.SemaphoreType.DMA((groups + 1, 2)),
                pltpu.SemaphoreType.DMA((groups + 1, 2)),
                pltpu.SemaphoreType.DMA((2 * blocks + 2,)),
            ],
            compiler_params=pltpu.CompilerParams(
                collective_id=0, has_side_effects=True, vmem_limit_bytes=48 << 20
            ),
        )(initial, source, diffusion, wind_field, buildings, strength)

    in_specs = (
        P(("copy", "tm"), "space", None, None),
        P(("copy", "tm"), "space", None, None),
        P("space", None, None),
        P(None, "space", None, None),
        P("space", None, None),
        P("tm", None),
    )
    out_specs = (P(("copy", "tm"), "space", None, None), P(("copy", "tm"), "space", None, None))
    return jax.shard_map(shards, mesh=mesh, in_specs=in_specs, out_specs=out_specs, check_vma=False)
```

time: 164 us -> 53.1 us (0.32)
  the two profiles are of different devices: /device:TPU:0 before, /device:TPU:1 now
where the time goes in v1:
time: 53.1 us; the launch traced here: 52.8 us
  Pallas kernels  45.6 us (86%)
  local copies, waits for them, and re-layouts  6.51 us (12%)
  between operations  0.65 us (1%)
    pallas_call x1, Pallas kernels, shards(): pl.pallas_call(functools.partial(kernel, slabs, blocks, rows, width, per,...  45.6 us
    unnamed x14, local copies, waits for them, and re-layouts  6.51 us

profile of v1, /device:TPU:1, one launch (start us, length us, event | category | flops | bytes accessed | tf_op | source)
XLA Modules:
  0.0 52.8 jit_solution(6288426118758764688)
XLA Ops:
  0.6 0.0 copy-start
  0.6 1.0 %copy-done = f32[3,2,128,128]{3,2,1,0:T(8,128)S(1)} copy-done((f32[3,2,128,128]{3,2,1,0:T(8,128)S(1)}, f32[3,2,128,128]{3,2,1,0:T(8,128)}, u32[]{:S(2)}) %copy-start) | copy-done | bytes 393240
  1.6 0.0 copy-start.1
  1.6 0.9 %copy-done.1 = f32[1,2,128,128]{3,2,1,0:T(8,128)S(1)} copy-done((f32[1,2,128,128]{3,2,1,0:T(8,128)S(1)}, f32[1,2,128,128]{3,2,1,0:T(8,128)}, u32[]{:S(2)}) %copy-start.1) | copy-done | bytes 131096
  2.5 0.0 copy-start.2
  2.5 0.9 %copy-done.2 = f32[2,128,128]{2,1,0:T(8,128)S(1)} copy-done((f32[2,128,128]{2,1,0:T(8,128)S(1)}, f32[2,128,128]{2,1,0:T(8,128)}, u32[]{:S(2)}) %copy-start.2) | copy-done | bytes 131096
  3.4 0.0 copy-start.3
  3.4 0.9 %copy-done.3 = s32[2,128,128]{2,1,0:T(8,128)S(1)} copy-done((s32[2,128,128]{2,1,0:T(8,128)S(1)}, s32[2,128,128]{2,1,0:T(8,128)}, u32[]{:S(2)}) %copy-start.3) | copy-done | bytes 131096
  4.3 0.0 copy-start.4
  4.3 0.8 %copy-done.4 = bf16[1,2,128,128]{3,2,1,0:T(8,128)(2,1)S(1)} copy-done((bf16[1,2,128,128]{3,2,1,0:T(8,128)(2,1)S(1)}, bf16[1,2,128,128]{3,2,1,0:T(8,128)(2,1)}, u32[]{:S(2)}) %copy-start.4) | copy-done | bytes 65560
  5.2 0.0 copy-start.5
  5.2 0.7 %copy-done.5 = f32[1,4]{1,0:T(1,128)S(1)} copy-done((f32[1,4]{1,0:T(1,128)S(1)}, f32[1,4]{1,0:T(1,128)}, u32[]{:S(2)}) %copy-start.5) | copy-done | bytes 40
  5.8 45.6 %shard_map.77 = (f32[1,2,128,128]{3,2,1,0:T(8,128)S(1)}, f32[1,2,128,128]{3,2,1,0:T(8,128)S(1)}) custom-call(f32[1,2,128,128]{3,2,1,0:T(8,128)S(1)} %copy-done.1, bf16[1,2,128,128]{3,2,1,0:T(8,128)(2,1)S(1)} %copy-done.4, f32[2,128,128]{2,1,0:T(8,128)S(1)} %copy-done.2, f32[3,2,128,128]{3,2,1,0:T(8,128)S(1)} %copy-done, s32[2,128,128]{2,1,0:T(8,128)S(1)} %copy-done.3, ...), custom_call_target="tpu_custom_call" | custom-call | tf_op jit(solution)/shard_map/pallas_call | solution.py:404
  51.5 0.7 %copy.10 = f32[1,2,128,128]{3,2,1,0:T(8,128)} copy(f32[1,2,128,128]{3,2,1,0:T(8,128)S(1)} %get-tuple-element.4) | data formatting | bytes 262144
  52.1 0.7 %copy.11 = f32[1,2,128,128]{3,2,1,0:T(8,128)} copy(f32[1,2,128,128]{3,2,1,0:T(8,128)S(1)} %get-tuple-element.5) | data formatting | bytes 262144
Async XLA Ops:
  0.6 1.0 %copy-start = (f32[3,2,128,128]{3,2,1,0:T(8,128)S(1)}, f32[3,2,128,128]{3,2,1,0:T(8,128)}, u32[]{:S(2)}) copy-start(f32[3,2,128,128]{3,2,1,0:T(8,128)} %wind_ref.1) | copy-start | bytes 1179652
  1.6 0.9 %copy-start.1 = (f32[1,2,128,128]{3,2,1,0:T(8,128)S(1)}, f32[1,2,128,128]{3,2,1,0:T(8,128)}, u32[]{:S(2)}) copy-start(f32[1,2,128,128]{3,2,1,0:T(8,128)} %initial_ref.1) | copy-start | bytes 393220
  2.5 0.9 %copy-start.2 = (f32[2,128,128]{2,1,0:T(8,128)S(1)}, f32[2,128,128]{2,1,0:T(8,128)}, u32[]{:S(2)}) copy-start(f32[2,128,128]{2,1,0:T(8,128)} %diffusion_ref.1) | copy-start | bytes 393220
  3.4 0.9 %copy-start.3 = (s32[2,128,128]{2,1,0:T(8,128)S(1)}, s32[2,128,128]{2,1,0:T(8,128)}, u32[]{:S(2)}) copy-start(s32[2,128,128]{2,1,0:T(8,128)} %buildings_ref.1) | copy-start | bytes 393220
  4.3 0.8 %copy-start.4 = (bf16[1,2,128,128]{3,2,1,0:T(8,128)(2,1)S(1)}, bf16[1,2,128,128]{3,2,1,0:T(8,128)(2,1)}, u32[]{:S(2)}) copy-start(bf16[1,2,128,128]{3,2,1,0:T(8,128)(2,1)} %source_ref.1) | copy-start | bytes 196612
  5.2 0.7 %copy-start.5 = (f32[1,4]{1,0:T(1,128)S(1)}, f32[1,4]{1,0:T(1,128)}, u32[]{:S(2)}) copy-start(f32[1,4]{1,0:T(1,128)} %strength_ref.1) | copy-start | bytes 52

commit v2 on v1

--- a/solution.py
+++ b/solution.py
@@ -130,20 +130,11 @@
     lax.fori_loop(1, cores, send_state, 0)
     pltpu.make_async_copy(sendc.at[mine], recvc.at[space], a2a_sem.at[1]).start()
     pltpu.make_async_copy(sends.at[mine], recvs.at[space * blocks + time], a2a_sem.at[3]).start()
-    drain(recvc, a2a_sem.at[1])
-    drain(recvs, a2a_sem.at[3])
 
     def turned(array):
         return jnp.swapaxes(array.reshape(nx, rows, nz), 0, 1)
 
     inside = slice(width, width + rows)
-    for field in range(4):
-        raw[field, inside] = turned(recvc[:, field])
-    for block in range(blocks):
-        for kind in range(2):
-            chunk = jnp.stack([recvs[s * blocks + block, kind] for s in range(slabs)])
-            raw[4 + kind * blocks + block, inside] = turned(chunk)
-
     last = cores - 1
 
     def swap(index, up_source, up_target, down_source, down_target):
@@ -187,11 +178,14 @@
             ref.at[:, width + rows : ext],
         )
 
-    swap(0, *views(raw))
-    raw_views = views(raw)
-    arrived(0, raw_views[1], raw_views[3])
+    drain(recvc, a2a_sem.at[1])
+    for field in range(4):
+        raw[field, inside] = turned(recvc[:, field])
+    coef_views = views(raw.at[0:4])
+    swap(0, *coef_views)
     for copy in rate_copy:
         copy.wait()
+    arrived(0, coef_views[1], coef_views[3])
 
     masked = raw[0]
     core_open = jnp.where(masked > 0.0, 1.0, 0.0)
@@ -250,6 +244,15 @@
 
     lax.fori_loop(1, cores, send_bound, 0)
 
+    drain(recvs, a2a_sem.at[3])
+    for block in range(blocks):
+        for kind in range(2):
+            chunk = jnp.stack([recvs[s * blocks + block, kind] for s in range(slabs)])
+            raw[4 + kind * blocks + block, inside] = turned(chunk)
+    state_views = views(raw.at[4 : 4 + 2 * blocks])
+    swap(1, *state_views)
+    arrived(1, state_views[1], state_views[3])
+
     def stencil(values, faces, axis_shift):
         inner = values[1:-1]
         first, second, third = faces
@@ -345,9 +348,9 @@
                 part.at[:, rows : rows + width], part.at[:, 0:width],
                 part.at[:, width : 2 * width], part.at[:, width + rows : ext],
             )
-            swap(exchange + 1, *cuts)
-            arrived(exchange + 1, cuts[1], cuts[3])
-            exchanges.append((exchange + 1, cuts))
+            swap(exchange + 2, *cuts)
+            arrived(exchange + 2, cuts[1], cuts[3])
+            exchanges.append((exchange + 2, cuts))
             for block in live:
                 current[block] = states[exchange, block]
             off = 0
@@ -373,7 +376,8 @@
 
     drain(back.at[0], out_sem.at[2 * blocks])
     unpack(advanced_ref, 0)
-    sent(0, raw_views[0], raw_views[2])
+    sent(0, coef_views[0], coef_views[2])
+    sent(1, state_views[0], state_views[2])
     for index, cuts in exchanges:
         sent(index, cuts[0], cuts[2])
     drain(recvc.at[0 : slabs - 1], a2a_sem.at[0])
@@ -396,7 +400,7 @@
         cores = slabs * blocks
         rows = ny // cores
         fine = strength.shape[1]
-        width = 4 if rows >= 4 else 2
+        width = 8 if rows >= 8 else 2
         per = width // 2
         groups = -(-(2 * fine - 1) // per) - 1
         ext = rows + 2 * width
@@ -404,7 +408,7 @@
         return pl.pallas_call(
             functools.partial(kernel, slabs, blocks, rows, width, per, groups),
             out_shape=[jax.ShapeDtypeStruct(initial.shape, f32)] * 2,
-            in_specs=[pl.BlockSpec(memory_space=pl.ANY)] * 5 + [pl.BlockSpec(memory_space=pltpu.SMEM)],
+            in_specs=[pl.BlockSpec(memory_space=pltpu.HBM)] * 5 + [pl.BlockSpec(memory_space=pltpu.SMEM)],
             out_specs=[pl.BlockSpec(memory_space=pltpu.VMEM)] * 2,
             scratch_shapes=[
                 pltpu.VMEM(initial.shape, f32),
@@ -426,12 +430,12 @@
                 pltpu.SemaphoreType.DMA((4,)),
                 pltpu.SemaphoreType.DMA((2,)),
                 pltpu.SemaphoreType.DMA((2,)),
-                pltpu.SemaphoreType.DMA((groups + 1, 2)),
-                pltpu.SemaphoreType.DMA((groups + 1, 2)),
+                pltpu.SemaphoreType.DMA((groups + 2, 2)),
+                pltpu.SemaphoreType.DMA((groups + 2, 2)),
                 pltpu.SemaphoreType.DMA((2 * blocks + 2,)),
             ],
             compiler_params=pltpu.CompilerParams(
-                collective_id=0, has_side_effects=True, vmem_limit_bytes=48 << 20
+                collective_id=0, has_side_effects=True, vmem_limit_bytes=63 << 20
             ),
         )(initial, source, diffusion, wind_field, buildings, strength)
 

time: 53.1 us -> 44 us (0.83)
  Pallas kernels: 45.6 us -> 40.9 us
  local copies, waits for them, and re-layouts: 6.51 us -> 2.26 us
    pallas_call x1, Pallas kernels: 45.6 us -> 40.9 us  [shards(): pl.pallas_call(functools.partial(kernel, slabs, blocks, rows, width, per,...]
    unnamed x14 -> x4, local copies, waits for them, and re-layouts: 6.51 us -> 2.26 us
where the time goes in v2:
time: 44 us; the launch traced here: 43.9 us
  Pallas kernels  40.9 us (93%)
  local copies, waits for them, and re-layouts  2.26 us (5%)
  between operations  0.65 us (1%)
    pallas_call x1, Pallas kernels, shards(): pl.pallas_call(functools.partial(kernel, slabs, blocks, rows, width, per,...  40.9 us
    unnamed x4, local copies, waits for them, and re-layouts  2.26 us

profile of v2, /device:TPU:1, one launch (start us, length us, event | category | flops | bytes accessed | tf_op | source)
XLA Modules:
  0.0 43.9 jit_solution(5142554140911454378)
XLA Ops:
  0.6 40.9 %shard_map.77 = (f32[1,2,128,128]{3,2,1,0:T(8,128)}, f32[1,2,128,128]{3,2,1,0:T(8,128)}) custom-call(f32[1,2,128,128]{3,2,1,0:T(8,128)} %initial_ref.1, bf16[1,2,128,128]{3,2,1,0:T(8,128)(2,1)} %source_ref.1, f32[2,128,128]{2,1,0:T(8,128)} %diffusion_ref.1, f32[3,2,128,128]{3,2,1,0:T(8,128)} %wind_ref.1, s32[2,128,128]{2,1,0:T(8,128)} %buildings_ref.1, ...), custom_call_target="tpu_custom_call" | custom-call | tf_op jit(solution)/shard_map/pallas_call | solution.py:408
  41.6 0.0 copy-start
  41.6 1.6 %copy.10 = f32[1,2,128,128]{3,2,1,0:T(8,128)} copy(f32[1,2,128,128]{3,2,1,0:T(8,128)} %get-tuple-element.4) | data formatting | bytes 262144
  43.2 0.0 copy-done
  43.2 0.7 %copy.11 = f32[1,2,128,128]{3,2,1,0:T(8,128)} copy(f32[1,2,128,128]{3,2,1,0:T(8,128)S(1)} %copy-done) | data formatting | bytes 262144
Async XLA Ops:
  41.6 1.6 %copy-start = (f32[1,2,128,128]{3,2,1,0:T(8,128)S(1)}, f32[1,2,128,128]{3,2,1,0:T(8,128)}, u32[]{:S(2)}) copy-start(f32[1,2,128,128]{3,2,1,0:T(8,128)} %get-tuple-element.5) | copy-start | bytes 393220

commit v3 on v2

--- a/solution.py
+++ b/solution.py
@@ -34,7 +34,7 @@
     slabs, blocks, rows, width, per, groups,
     initial_ref, source_ref, diffusion_ref, wind_ref, buildings_ref, strength_ref,
     advanced_ref, final_ref,
-    initial, source, diffusion, wind, buildings,
+    initial, source, diffusion, wind, buildings, strength,
     sendc, sends, recvc, recvs, raw, states, rates, gath, outs, back,
     load_sem, a2a_sem, rate_sem, gath_sem, halo_send, halo_recv, out_sem,
 ):
@@ -59,6 +59,7 @@
                 (wind_ref, wind),
                 (initial_ref, initial),
                 (source_ref, source),
+                (strength_ref, strength),
             )
         )
     ]
@@ -72,8 +73,6 @@
         for block in range(blocks):
             states[index, block, 0:width] = blank
             states[index, block, width + rows : ext] = blank
-    for k in range(fine):
-        rates[time, k] = jnp.full((8, nz), strength_ref[0, k], jnp.float32)
 
     barrier = pltpu.get_barrier_semaphore()
 
@@ -93,6 +92,8 @@
 
     for load in loads:
         load.wait()
+    for k in range(fine):
+        rates[time, k] = jnp.broadcast_to(strength[0:1, k : k + 1], (8, nz))
     opened = (1 - buildings[...]).astype(jnp.float32)
     pack(sendc, 0, diffusion[...] * opened)
     for axis in range(3):
@@ -292,6 +293,18 @@
         j = block * fine + k
         return values[2:-2] + alpha[j : j + 1] * inner - beta[j : j + 1] * applied
 
+    def landing(kind):
+        target = (advanced_ref, final_ref)[kind]
+        if rows % 8 == 0:
+            return target.at[0, :, pl.ds(pl.multiple_of(mine * rows, 8), rows)]
+        return back.at[kind, mine]
+
+    def landed(kind):
+        target = (advanced_ref, final_ref)[kind]
+        drain(target if rows % 8 == 0 else back.at[kind], out_sem.at[2 * blocks + kind])
+        if rows % 8:
+            unpack(target, kind)
+
     def deliver(slot, owner_block, value):
         outs[slot] = jnp.swapaxes(value, 0, 1).reshape(slabs, layers, rows, nz)
         kind = slot // blocks
@@ -299,7 +312,7 @@
         def send(step, _):
             target = (space + step) % slabs
             pltpu.make_async_remote_copy(
-                outs.at[slot, target], back.at[kind, mine], out_sem.at[slot], out_sem.at[2 * blocks + kind],
+                outs.at[slot, target], landing(kind), out_sem.at[slot], out_sem.at[2 * blocks + kind],
                 device_id={"space": target, "tm": owner_block}, device_id_type=MESH,
             ).start()
             return 0
@@ -309,13 +322,13 @@
         @pl.when(time == owner_block)
         def _():
             pltpu.make_async_copy(
-                outs.at[slot, space], back.at[kind, mine], out_sem.at[2 * blocks + kind]
+                outs.at[slot, space], landing(kind), out_sem.at[2 * blocks + kind]
             ).start()
 
         @pl.when(time != owner_block)
         def _():
             pltpu.make_async_remote_copy(
-                outs.at[slot, space], back.at[kind, mine], out_sem.at[slot], out_sem.at[2 * blocks + kind],
+                outs.at[slot, space], landing(kind), out_sem.at[slot], out_sem.at[2 * blocks + kind],
                 device_id={"tm": owner_block}, device_id_type=MESH,
             ).start()
 
@@ -368,14 +381,10 @@
 
     def unpack(dest, kind):
         for layer in range(layers):
-            if rows % 8 == 0:
-                dest[0, layer] = back[kind, :, layer].reshape(ny, nz)
-            else:
-                for core in range(cores):
-                    dest[0, layer, core * rows : (core + 1) * rows] = back[kind, core, layer]
-
-    drain(back.at[0], out_sem.at[2 * blocks])
-    unpack(advanced_ref, 0)
+            for core in range(cores):
+                dest[0, layer, core * rows : (core + 1) * rows] = back[kind, core, layer]
+
+    landed(0)
     sent(0, coef_views[0], coef_views[2])
     sent(1, state_views[0], state_views[2])
     for index, cuts in exchanges:
@@ -386,8 +395,7 @@
     for kind in range(2):
         for block in range(blocks):
             settled(kind * blocks + block, block)
-    drain(back.at[1], out_sem.at[2 * blocks + 1])
-    unpack(final_ref, 1)
+    landed(1)
 
 
 def solution(mesh):
@@ -408,14 +416,15 @@
         return pl.pallas_call(
             functools.partial(kernel, slabs, blocks, rows, width, per, groups),
             out_shape=[jax.ShapeDtypeStruct(initial.shape, f32)] * 2,
-            in_specs=[pl.BlockSpec(memory_space=pltpu.HBM)] * 5 + [pl.BlockSpec(memory_space=pltpu.SMEM)],
-            out_specs=[pl.BlockSpec(memory_space=pltpu.VMEM)] * 2,
+            in_specs=[pl.BlockSpec(memory_space=pltpu.HBM)] * 6,
+            out_specs=[pl.BlockSpec(memory_space=pltpu.HBM if rows % 8 == 0 else pltpu.VMEM)] * 2,
             scratch_shapes=[
                 pltpu.VMEM(initial.shape, f32),
                 pltpu.VMEM(source.shape, source.dtype),
                 pltpu.VMEM(diffusion.shape, f32),
                 pltpu.VMEM(wind_field.shape, f32),
                 pltpu.VMEM(buildings.shape, buildings.dtype),
+                pltpu.VMEM(strength.shape, f32),
                 pltpu.VMEM((cores, 4, layers, rows, nz), f32),
                 pltpu.VMEM((cores, 2, layers, rows, nz), f32),
                 pltpu.VMEM((slabs, 4, layers, rows, nz), f32),
@@ -425,8 +434,8 @@
                 pltpu.VMEM((blocks, fine, 8, nz), f32),
                 pltpu.VMEM((cores, blocks * fine, nz), f32),
                 pltpu.VMEM((2 * blocks, slabs, layers, rows, nz), f32),
-                pltpu.VMEM((2, cores, layers, rows, nz), f32),
-                pltpu.SemaphoreType.DMA((5,)),
+                pltpu.VMEM((2, cores if rows % 8 else 1, layers, rows, nz), f32),
+                pltpu.SemaphoreType.DMA((6,)),
                 pltpu.SemaphoreType.DMA((4,)),
                 pltpu.SemaphoreType.DMA((2,)),
                 pltpu.SemaphoreType.DMA((2,)),

time: 44 us -> 42.8 us (0.973)
  Pallas kernels: 40.9 us -> 39.7 us
    pallas_call x1, Pallas kernels: 40.9 us -> 39.7 us  [shards(): pl.pallas_call(functools.partial(kernel, slabs, blocks, rows, width, per,...]
where the time goes in v3:
time: 42.8 us; the launch traced here: 42.6 us
  Pallas kernels  39.7 us (93%)
  local copies, waits for them, and re-layouts  2.26 us (5%)
  between operations  0.65 us (2%)
    pallas_call x1, Pallas kernels, shards(): pl.pallas_call(functools.partial(kernel, slabs, blocks, rows, width, per,...  39.7 us
    unnamed x4, local copies, waits for them, and re-layouts  2.26 us

profile of v3, /device:TPU:1, one launch (start us, length us, event | category | flops | bytes accessed | tf_op | source)
XLA Modules:
  0.0 42.6 jit_solution(15730773474130628394)
XLA Ops:
  0.6 39.7 %shard_map.77 = (f32[1,2,128,128]{3,2,1,0:T(8,128)}, f32[1,2,128,128]{3,2,1,0:T(8,128)}) custom-call(f32[1,2,128,128]{3,2,1,0:T(8,128)} %initial_ref.1, bf16[1,2,128,128]{3,2,1,0:T(8,128)(2,1)} %source_ref.1, f32[2,128,128]{2,1,0:T(8,128)} %diffusion_ref.1, f32[3,2,128,128]{3,2,1,0:T(8,128)} %wind_ref.1, s32[2,128,128]{2,1,0:T(8,128)} %buildings_ref.1, ...), custom_call_target="tpu_custom_call" | custom-call | tf_op jit(solution)/shard_map/pallas_call | solution.py:416
  40.3 0.0 copy-start
  40.3 1.6 %copy.10 = f32[1,2,128,128]{3,2,1,0:T(8,128)} copy(f32[1,2,128,128]{3,2,1,0:T(8,128)} %get-tuple-element.4) | data formatting | bytes 262144
  41.9 0.0 copy-done
  41.9 0.7 %copy.11 = f32[1,2,128,128]{3,2,1,0:T(8,128)} copy(f32[1,2,128,128]{3,2,1,0:T(8,128)S(1)} %copy-done) | data formatting | bytes 262144
Async XLA Ops:
  40.3 1.6 %copy-start = (f32[1,2,128,128]{3,2,1,0:T(8,128)S(1)}, f32[1,2,128,128]{3,2,1,0:T(8,128)}, u32[]{:S(2)}) copy-start(f32[1,2,128,128]{3,2,1,0:T(8,128)} %get-tuple-element.5) | copy-start | bytes 393220
